TPU v7x, 512 devices: a whole 4x8x8 slice. The times are simulated.
512 devices in a mesh: dp: 32 (over z, x_hi, core), fsdp: 16 (over x_lo, y).
Axes of the slice: x: 4 (x_hi: 2, x_lo: 2; x = x_hi * 2 + x_lo), y: 8, z: 8, core: 2. Of those that a mesh axis runs over, the one named last changes fastest.
Arguments:
- activations: bfloat16 [98304, 4096], P(('dp', 'fsdp')), may hold values from -24 to 24
- cotangent: bfloat16 [98304, 512], P(('dp', 'fsdp')), may hold values from -6 to 6
- weight: bfloat16 [4096, 512], P('fsdp'), may hold values from -0.09375 to 0.09375
- momentum: float32 [32, 4096, 512], P('dp', 'fsdp'), may hold values from -256 to 256
- positions: int32 [16, 32, 512], P('fsdp'), may hold values from 0 to 255, as said below
Outputs:
- grad_input: bfloat16 [98304, 4096], P(('dp', 'fsdp'))
- new_momentum: float32 [32, 4096, 512], P('dp', 'fsdp')
- update: bfloat16 [4096, 512], P('fsdp')
Inputs may be any that keep to these rules, and one draw needn't show every extreme that they name: For each block b and column c the 32 values positions[b, :, c] are distinct.
All inputs are finite; a program needn't handle non-finite values.
Results may differ from a plain program's by a relative error of at most 0.023.
Values may be sent and summed in bfloat16 or wider, within the bound.
A program may use at most 64 MiB of HBM per device.

v0:
```python
import math
import jax
import jax.numpy as jnp
from jax import lax
from jax.sharding import PartitionSpec as P

SPAN = 256
MOMENTUM_DECAY = 0.999


def transform_table(length):
    freq = jnp.arange(length, dtype=jnp.float32)[:, None]
    place = jnp.arange(length, dtype=jnp.float32)[None, :]
    angles = jnp.pi * (2.0 * place + 1.0) * freq / (2.0 * length)
    scales = jnp.where(freq == 0.0, jnp.sqrt(1.0 / length), jnp.sqrt(2.0 / length))
    return scales * jnp.cos(angles)


def forward_blocks(table, blocks):
    return jnp.einsum("kn,bnc->bkc", table, blocks, precision=lax.Precision.HIGHEST)


def inverse_blocks(table, coeffs):
    return jnp.einsum("kn,bkc->bnc", table, coeffs, precision=lax.Precision.HIGHEST)


def grouped_positions(positions):
    blocks, picks, columns = positions.shape
    group = math.gcd(picks, 8)
    stacked = positions.reshape(blocks, picks // group, group, columns)
    return (jnp.transpose(stacked, (1, 0, 2, 3)), group)


def pick_band(coeffs, positions):
    blocks, length, columns = coeffs.shape
    picks = positions.shape[1]
    stacked, group = grouped_positions(positions)
    levels = jnp.arange(length, dtype=jnp.int32)[None, None, :, None]

    def one_group(where):
        onehot = where[:, :, None, :] == levels
        return jnp.sum(jnp.where(onehot, coeffs[:, None, :, :], 0.0), axis=2)

    found = lax.map(one_group, stacked)
    return jnp.transpose(found, (1, 0, 2, 3)).reshape(blocks, picks, columns)


def place_band(values, positions, length):
    blocks, picks, columns = values.shape
    stacked, group = grouped_positions(positions)
    stacked_values = jnp.transpose(
        values.reshape(blocks, picks // group, group, columns), (1, 0, 2, 3)
    )
    levels = jnp.arange(length, dtype=jnp.int32)[None, None, :, None]

    def add_group(dense, packed):
        where, amounts = packed
        onehot = where[:, :, None, :] == levels
        return (dense + jnp.sum(jnp.where(onehot, amounts[:, :, None, :], 0.0), axis=1), None)

    start = jnp.zeros((blocks, length, columns), jnp.float32)
    dense, unused = lax.scan(add_group, start, (stacked, stacked_values))
    return dense


def contract_last(left, right):
    return lax.dot_general(
        left, right, (((1,), (1,)), ((), ())), preferred_element_type=jnp.float32
    )


def on_device(activations, cotangent, weight, momentum, positions):
    table = transform_table(SPAN)
    grad_input = contract_last(
        cotangent, lax.all_gather(weight, "fsdp", axis=0, tiled=True)
    ).astype(jnp.bfloat16)
    gradient = lax.psum_scatter(
        lax.dot_general(
            activations, cotangent, (((0,), (0,)), ((), ())), preferred_element_type=jnp.float32
        ).astype(jnp.bfloat16),
        "fsdp",
        scatter_dimension=0,
        tiled=True,
    ).astype(jnp.float32)
    moment = MOMENTUM_DECAY * momentum[0] + gradient
    blocks = moment.reshape(positions.shape[0], SPAN, moment.shape[1])
    coeffs = forward_blocks(table, blocks)
    picked = pick_band(coeffs, positions)
    kept = blocks - inverse_blocks(table, place_band(picked, positions, SPAN))
    new_momentum = kept.reshape(moment.shape)[None]
    bands = picked.astype(jnp.bfloat16)
    replicas = lax.axis_size("dp")
    summed = jnp.sum(
        lax.all_gather(bands[None], "dp", axis=0, tiled=True).astype(jnp.float32), axis=0
    )
    mean_band = summed / replicas
    update = (
        inverse_blocks(table, place_band(mean_band, positions, SPAN))
        .reshape(moment.shape)
        .astype(jnp.bfloat16)
    )
    return (grad_input, new_momentum, update)


def solution(mesh):
    placed = (
        P(("dp", "fsdp"), None),
        P(("dp", "fsdp"), None),
        P("fsdp", None),
        P("dp", "fsdp", None),
        P("fsdp", None, None),
    )
    return jax.shard_map(
        on_device,
        mesh=mesh,
        in_specs=placed,
        out_specs=(P(("dp", "fsdp"), None), P("dp", "fsdp", None), P("fsdp", None)),
        check_vma=False,
    )
```

profile of v0, /device:TPU:1, one launch (start us, length us, event | category | flops | bytes accessed | tf_op | source)
XLA Modules:
  0.0 280.2 jit_solution(7000928409608363338)
XLA Ops:
  7.2 0.7 all-gather.3.cloned.1.call-update
  8.0 0.6 copy-done
  8.6 4.2 %convolution_convert_fusion = bf16[4096,512]{1,0:T(8,128)(2,1)} fusion(bf16[192,4096]{1,0:T(8,128)(2,1)S(1)} %copy-done, bf16[192,512]{1,0:T(8,128)(2,1)} %param.12), kind=kOutput, calls=%fused_computation.17 | convolution fusion | flops 807403520 | bytes 5963776 | tf_op jit(solution)/shard_map/dot_general | solution.py:78
  12.9 73.1 %all-gather.3.cloned.1.call-done = bf16[4096,512]{1,0:T(8,128)(2,1)} async-done(((bf16[256,512]{1,0:T(8,128)(2,1)}), bf16[4096,512]{1,0:T(8,128)(2,1)}) %all-gather.3.cloned.1.call-update) | async-done | bytes 4194320 | tf_op jit(solution)/shard_map/all_gather | solution.py:75
  86.0 4.8 %convolution_convert_fusion.1 = bf16[192,4096]{1,0:T(8,128)(2,1)} fusion(bf16[192,512]{1,0:T(8,128)(2,1)S(1)} %copy-done.4, bf16[4096,512]{1,0:T(8,128)(2,1)} %all-gather.3.cloned.1.call-done), kind=kOutput, calls=%fused_computation.18 | convolution fusion | flops 806092800 | bytes 5963776 | tf_op jit(solution)/shard_map/dot_general | solution.py:67
  90.9 77.3 %reduce-scatter.2.cloned.1.call-done = bf16[256,512]{1,0:T(8,128)(2,1)} async-done(((bf16[4096,512]{1,0:T(8,128)(2,1)}), bf16[256,512]{1,0:T(8,128)(2,1)}) %reduce-scatter.2.cloned.1.call-update) | async-done | bytes 262160 | tf_op jit(solution)/shard_map/reduce_scatter | solution.py:77
  168.2 3.6 %convolution_bitcast_fusion.1 = f32[1,256,512]{1,2,0:T(8,128)} fusion(bf16[256,512]{1,0:T(8,128)(2,1)} %reduce-scatter.2.cloned.1.call-done, f32[1,256,512]{2,1,0:T(8,128)S(1)} %copy-done.1, f32[256]{0:T(256)S(1)} %get-tuple-element.184, f32[256]{0:T(256)S(1)} %get-tuple-element.183), kind=kOutput, calls=%fused_computation.21 | convolution fusion | flops 403243008 | bytes 1312768 | tf_op jit(solution)/shard_map/kn,bnc->bkc/dot_general | solution.py:20
  171.8 1.2 copy.17
  173.1 2.1 while.33
  173.1 0.5 select_reduce_fusion.6
  173.6 0.5 select_reduce_fusion.6
  174.1 0.5 select_reduce_fusion.6
  174.7 0.5 select_reduce_fusion.6
  175.2 0.6 convert_bitcast_fusion
  175.8 3.1 %while.34 = (s32[]{:T(128)}, f32[1,256,512]{2,1,0:T(8,128)S(1)}, s32[4,1,8,512]{3,2,1,0:T(8,128)S(1)}, f32[4,1,8,512]{3,2,1,0:T(8,128)S(1)}, s32[]{:T(128)}, /*index=5*/s32[]{:T(128)}) while((s32[]{:T(128)}, f32[1,256,512]{2,1,0:T(8,128)S(1)}, s32[4,1,8,512]{3,2,1,0:T(8,128)S(1)}, f32[4,1,8,512]{3,2,1,0:T(8,128)S(1)}, s32[]{:T(128)}, ...), condition=%wide.region_6.7_spmd.clone, body=%wide.region_4.6_spmd.clone.sunk | while | flops 3276803 | bytes 2195543 | solution.py:62
  175.9 0.5 select_reduce_fusion.7
  176.4 0.2 bitcast_add_fusion.6
  176.6 0.5 select_reduce_fusion.7
  177.2 0.2 bitcast_add_fusion.6
  177.4 0.5 select_reduce_fusion.7
  178.2 0.5 select_reduce_fusion.7
  178.9 3.4 %fusion.6 = f32[1,256,512]{2,1,0:T(8,128)} fusion(f32[1,256,512]{2,1,0:T(8,128)S(1)} %get-tuple-element.85, bf16[256,512]{1,0:T(8,128)(2,1)S(1)} %copy-done.2, f32[1,256,512]{2,1,0:T(8,128)} %param.14, f32[256]{0:T(256)S(1)} %get-tuple-element.184, f32[256]{0:T(256)S(1)} %get-tuple-element.183), kind=kOutput, calls=%fused_computation.22 | convolution fusion | flops 403374080 | bytes 1837056 | tf_op jit(solution)/shard_map/kn,bkc->bnc/dot_general | solution.py:24
  182.4 84.1 %all-gather.5.cloned.1.call-done = bf16[32,1,32,512]{3,2,1,0:T(8,128)(2,1)} async-done(((bf16[1,1,32,512]{3,2,1,0:T(8,128)(2,1)}), bf16[32,1,32,512]{3,2,1,0:T(8,128)(2,1)}) %all-gather.5.cloned.1.call-update) | async-done | bytes 1048592 | tf_op jit(solution)/shard_map/all_gather | solution.py:94
  266.5 1.4 convert_reduce_fusion
  267.9 3.1 %while.35 = (s32[]{:T(128)}, f32[1,256,512]{2,1,0:T(8,128)S(1)}, s32[4,1,8,512]{3,2,1,0:T(8,128)S(1)}, f32[4,1,8,512]{3,2,1,0:T(8,128)S(1)}, s32[]{:T(128)}, /*index=5*/s32[]{:T(128)}) while((s32[]{:T(128)}, f32[1,256,512]{2,1,0:T(8,128)S(1)}, s32[4,1,8,512]{3,2,1,0:T(8,128)S(1)}, f32[4,1,8,512]{3,2,1,0:T(8,128)S(1)}, ...), condition=%wide.region_10.11_spmd.clone, body=%wide.region_8.10_spmd.clone.sunk | while | flops 3276803 | bytes 2195543 | solution.py:62
  267.9 0.5 select_reduce_fusion.8
  268.7 0.5 select_reduce_fusion.8
  269.5 0.5 select_reduce_fusion.8
  270.0 0.2 bitcast_add_fusion.7
  270.2 0.5 select_reduce_fusion.8
  271.0 1.8 fusion.7
  272.8 0.8 copy.19
  (48 shorter events, 1.3 us)
Async XLA Ops:
  7.2 1.4 copy-start
  7.2 78.8 %all-gather.3.cloned.1.call-start = ((), (), s32[]{:S(2)}) async-start(), calls=%async_computation.1 | async-start | bytes 4456448 | tf_op jit(solution)/shard_map/all_gather | solution.py:75
  7.9 160.3 %reduce-scatter.2.cloned.1.call-start = ((), (), s32[]{:S(2)}) async-start(), calls=%async_computation.2 | async-start | bytes 4456448 | tf_op jit(solution)/shard_map/reduce_scatter | solution.py:77
  12.8 73.3 %copy-start.4 = (bf16[192,512]{1,0:T(8,128)(2,1)S(1)}, bf16[192,512]{1,0:T(8,128)(2,1)}, u32[]{:S(2)}) copy-start(bf16[192,512]{1,0:T(8,128)(2,1)} %param.12) | copy-start | bytes 589828
  12.8 155.4 %copy-start.1 = (f32[1,256,512]{2,1,0:T(8,128)S(1)}, f32[1,256,512]{2,1,0:T(8,128)}, u32[]{:S(2)}) copy-start(f32[1,256,512]{2,1,0:T(8,128)} %param.14) | copy-start | bytes 1572868
  12.8 160.3 %copy-start.3 = (s32[1,32,512]{2,1,0:T(8,128)S(1)}, s32[1,32,512]{2,1,0:T(8,128)}, u32[]{:S(2)}) copy-start(s32[1,32,512]{2,1,0:T(8,128)} %param.15) | copy-start | bytes 196612
  12.8 253.6 %all-gather.5.cloned.1.call-start = ((), (), s32[]{:S(2)}) async-start(), calls=%async_computation.3 | async-start | bytes 1081344 | tf_op jit(solution)/shard_map/all_gather | solution.py:94
  175.8 3.1 %copy-start.2 = (bf16[256,512]{1,0:T(8,128)(2,1)S(1)}, bf16[256,512]{1,0:T(8,128)(2,1)}, u32[]{:S(2)}) copy-start(bf16[256,512]{1,0:T(8,128)(2,1)} %reduce-scatter.2.cloned.1.call-done) | copy-start | bytes 786436
Sparse Core Ops, SparseCore 0:
  10.1 75.8 all-gather.2
  88.9 79.2 reduce-scatter.1
  175.9 90.4 all-gather.4
where the time goes:
time: 281 us; the launch traced here: 280 us
  waiting for transfers between devices  235 us (84%)
  matrix products  17.9 us (6%)
  between operations  13.9 us (5%)
  other arithmetic  9.54 us (3%)
  local copies, waits for them, and re-layouts  2.94 us (1%)
    all_gather x1, waiting for transfers between devices, on_device(): lax.all_gather(bands[None], 'dp', axis=0, tiled=True).astype(jnp.float32)  84.1 us
    reduce_scatter x1, waiting for transfers between devices, on_device(): lax.psum_scatter(lax.dot_general(activations, cotangent, (((0,), (0,)), (...  77.3 us
    all_gather x1, waiting for transfers between devices, on_device(): lax.all_gather(weight, 'fsdp', axis=0, tiled=True)  73.1 us
  transfers between devices with their start and end apart: 3, of which 3 were waited for; matrix products, arithmetic and copies ran while one was open for 5% of the time, Pallas kernels for 0%

commit v1 on v0

--- a/solution.py
+++ b/solution.py
@@ -6,6 +6,13 @@
 
 SPAN = 256
 MOMENTUM_DECAY = 0.999
+
+
+def exchange_gather(array, axis, dim):
+    size = lax.axis_size(axis)
+    pieces = jnp.stack([array for _ in range(size)])
+    pieces = lax.all_to_all(pieces, axis, split_axis=0, concat_axis=0)
+    return jnp.concatenate(pieces, axis=dim)
 
 
 def transform_table(length):
@@ -90,9 +97,7 @@
     new_momentum = kept.reshape(moment.shape)[None]
     bands = picked.astype(jnp.bfloat16)
     replicas = lax.axis_size("dp")
-    summed = jnp.sum(
-        lax.all_gather(bands[None], "dp", axis=0, tiled=True).astype(jnp.float32), axis=0
-    )
+    summed = jnp.sum(exchange_gather(bands[None], "dp", 0).astype(jnp.float32), axis=0)
     mean_band = summed / replicas
     update = (
         inverse_blocks(table, place_band(mean_band, positions, SPAN))

time: 281 us -> 239 us (0.85)
  waiting for transfers between devices: 235 us -> 173 us
  starting transfers between devices: 0.12 us -> 20.3 us
    all_gather x1 -> x0, waiting for transfers between devices: 84.1 us -> none  [on_device(): lax.all_gather(bands[None], 'dp', axis=0, tiled=True).astype(jnp.float32)]
    all_to_all x0 -> x1, waiting for transfers between devices: none -> 21.6 us  [exchange_gather(): pieces = lax.all_to_all(pieces, axis, split_axis=0, concat_axis=0)]
    all_to_all x0 -> x1, starting transfers between devices: none -> 20.2 us  [exchange_gather(): pieces = lax.all_to_all(pieces, axis, split_axis=0, concat_axis=0)]
  transfers between devices with their start and end apart: 3 -> 3, of which waited for: 3 -> 3; matrix products, arithmetic and copies ran while one was open for 5% -> 6% of each run, Pallas kernels for 0% -> 0%
where the time goes in v1:
time: 239 us
  waiting for transfers between devices  173 us (72%)
  starting transfers between devices  20.3 us (8%)
  matrix products  17.9 us (7%)
  between operations  14.2 us (6%)
  other arithmetic  8.93 us (4%)
  local copies, waits for them, and re-layouts  4.08 us (2%)
    reduce_scatter x1, waiting for transfers between devices, on_device(): lax.psum_scatter(lax.dot_general(activations, cotangent, (((0,), (0,)), (...  77.3 us
    all_gather x1, waiting for transfers between devices, on_device(): lax.all_gather(weight, 'fsdp', axis=0, tiled=True)  73.2 us
    all_to_all x1, waiting for transfers between devices, exchange_gather(): pieces = lax.all_to_all(pieces, axis, split_axis=0, concat_axis=0)  21.6 us
    all_to_all x1, starting transfers between devices, exchange_gather(): pieces = lax.all_to_all(pieces, axis, split_axis=0, concat_axis=0)  20.2 us
    dot_general x2, matrix products, inverse_blocks(): jnp.einsum('kn,bkc->bnc', table, coeffs, precision=lax.Precision.HIGHEST)  5.26 us
    dot_general x1, matrix products, contract_last(): lax.dot_general(left, right, (((1,), (1,)), ((), ())), preferred_element_...  4.84 us
  transfers between devices with their start and end apart: 3, of which 3 were waited for; matrix products, arithmetic and copies ran while one was open for 6% of the time, Pallas kernels for 0%

profile of v1, /device:TPU:1, one launch (start us, length us, event | category | flops | bytes accessed | tf_op | source)
XLA Modules:
  0.0 238.7 jit_solution(5416888851404773736)
XLA Ops:
  7.2 0.7 all-gather.2.cloned.1.call-update
  8.0 0.6 copy-done
  8.6 4.2 %convolution_convert_fusion = bf16[4096,512]{1,0:T(8,128)(2,1)} fusion(bf16[192,4096]{1,0:T(8,128)(2,1)S(1)} %copy-done, bf16[192,512]{1,0:T(8,128)(2,1)} %param.12), kind=kOutput, calls=%fused_computation.17 | convolution fusion | flops 807403520 | bytes 5963776 | tf_op jit(solution)/shard_map/dot_general | solution.py:85
  12.9 73.2 %all-gather.2.cloned.1.call-done = bf16[4096,512]{1,0:T(8,128)(2,1)} async-done(((bf16[256,512]{1,0:T(8,128)(2,1)}), bf16[4096,512]{1,0:T(8,128)(2,1)}) %all-gather.2.cloned.1.call-update) | async-done | bytes 4194320 | tf_op jit(solution)/shard_map/all_gather | solution.py:82
  86.0 4.8 %convolution_convert_fusion.1 = bf16[192,4096]{1,0:T(8,128)(2,1)} fusion(bf16[192,512]{1,0:T(8,128)(2,1)S(1)} %copy-done.4, bf16[4096,512]{1,0:T(8,128)(2,1)} %all-gather.2.cloned.1.call-done), kind=kOutput, calls=%fused_computation.18 | convolution fusion | flops 806092800 | bytes 5963776 | tf_op jit(solution)/shard_map/dot_general | solution.py:74
  90.9 77.3 %reduce-scatter.2.cloned.1.call-done = bf16[256,512]{1,0:T(8,128)(2,1)} async-done(((bf16[4096,512]{1,0:T(8,128)(2,1)}), bf16[256,512]{1,0:T(8,128)(2,1)}) %reduce-scatter.2.cloned.1.call-update) | async-done | bytes 262160 | tf_op jit(solution)/shard_map/reduce_scatter | solution.py:84
  168.2 3.6 %convolution_bitcast_fusion.1 = f32[1,256,512]{1,2,0:T(8,128)} fusion(bf16[256,512]{1,0:T(8,128)(2,1)} %reduce-scatter.2.cloned.1.call-done, f32[1,256,512]{2,1,0:T(8,128)S(1)} %copy-done.1, f32[256]{0:T(256)S(1)} %get-tuple-element.181, f32[256]{0:T(256)S(1)} %get-tuple-element.180), kind=kOutput, calls=%fused_computation.21 | convolution fusion | flops 403243008 | bytes 1312768 | tf_op jit(solution)/shard_map/kn,bnc->bkc/dot_general | solution.py:27
  171.8 1.2 copy.14
  173.1 2.1 while.33
  173.1 0.5 select_reduce_fusion.6
  173.6 0.5 select_reduce_fusion.6
  174.1 0.5 select_reduce_fusion.6
  174.7 0.5 select_reduce_fusion.6
  175.2 1.1 stack.3
  176.3 20.2 %all-to-all-start = ((bf16[32,1,1,32,512]{4,3,2,1,0:T(8,128)(2,1)}), bf16[32,1,1,32,512]{4,3,2,1,0:T(8,128)(2,1)}, u32[]{:S(2)}, u32[]{:S(2)}) async-start(bf16[32,1,1,32,512]{4,3,2,1,0:T(8,128)(2,1)} %stack.3), calls=%async_computation.1 | async-start | bytes 2097152 | tf_op jit(solution)/shard_map/all_to_all | solution.py:14
  196.6 3.1 %while.34 = (s32[]{:T(128)}, f32[1,256,512]{2,1,0:T(8,128)S(1)}, s32[4,1,8,512]{3,2,1,0:T(8,128)S(1)}, f32[4,1,8,512]{3,2,1,0:T(8,128)S(1)}, s32[]{:T(128)}, /*index=5*/s32[]{:T(128)}) while((s32[]{:T(128)}, f32[1,256,512]{2,1,0:T(8,128)S(1)}, s32[4,1,8,512]{3,2,1,0:T(8,128)S(1)}, f32[4,1,8,512]{3,2,1,0:T(8,128)S(1)}, s32[]{:T(128)}, ...), condition=%wide.region_6.7_spmd.clone, body=%wide.region_4.6_spmd.clone.sunk | while | flops 3276803 | bytes 2195543 | solution.py:69
  196.6 0.5 select_reduce_fusion.7
  197.1 0.2 bitcast_add_fusion.6
  197.4 0.5 select_reduce_fusion.7
  197.9 0.2 bitcast_add_fusion.6
  198.1 0.5 select_reduce_fusion.7
  198.9 0.5 select_reduce_fusion.7
  199.7 3.4 %fusion.6 = f32[1,256,512]{2,1,0:T(8,128)} fusion(f32[1,256,512]{2,1,0:T(8,128)S(1)} %get-tuple-element.85, bf16[256,512]{1,0:T(8,128)(2,1)S(1)} %copy-done.2, f32[1,256,512]{2,1,0:T(8,128)} %param.14, f32[256]{0:T(256)S(1)} %get-tuple-element.181, f32[256]{0:T(256)S(1)} %get-tuple-element.180), kind=kOutput, calls=%fused_computation.22 | convolution fusion | flops 403374080 | bytes 1837056 | tf_op jit(solution)/shard_map/kn,bkc->bnc/dot_general | solution.py:31
  203.1 21.6 %all-to-all-done = bf16[32,1,1,32,512]{4,3,2,1,0:T(8,128)(2,1)} async-done(((bf16[32,1,1,32,512]{4,3,2,1,0:T(8,128)(2,1)}), bf16[32,1,1,32,512]{4,3,2,1,0:T(8,128)(2,1)}, u32[]{:S(2)}, u32[]{:S(2)}) %all-to-all-start) | async-done | bytes 1048608 | tf_op jit(solution)/shard_map/all_to_all | solution.py:14
  224.7 1.4 convert_reduce_fusion
  226.1 3.1 %while.35 = (s32[]{:T(128)}, f32[1,256,512]{2,1,0:T(8,128)S(1)}, s32[4,1,8,512]{3,2,1,0:T(8,128)S(1)}, f32[4,1,8,512]{3,2,1,0:T(8,128)S(1)}, s32[]{:T(128)}, /*index=5*/s32[]{:T(128)}) while((s32[]{:T(128)}, f32[1,256,512]{2,1,0:T(8,128)S(1)}, s32[4,1,8,512]{3,2,1,0:T(8,128)S(1)}, f32[4,1,8,512]{3,2,1,0:T(8,128)S(1)}, ...), condition=%wide.region_10.11_spmd.clone, body=%wide.region_8.10_spmd.clone.sunk | while | flops 3276803 | bytes 2195543 | solution.py:69
  226.2 0.5 select_reduce_fusion.8
  226.9 0.5 select_reduce_fusion.8
  227.7 0.5 select_reduce_fusion.8
  228.5 0.5 select_reduce_fusion.8
  229.2 1.8 fusion.7
  231.1 0.8 copy.17
  (48 shorter events, 1.4 us)
Async XLA Ops:
  7.2 1.4 copy-start
  7.2 78.8 %all-gather.2.cloned.1.call-start = ((), (), s32[]{:S(2)}) async-start(), calls=%async_computation.2 | async-start | bytes 4456448 | tf_op jit(solution)/shard_map/all_gather | solution.py:82
  7.9 160.3 %reduce-scatter.2.cloned.1.call-start = ((), (), s32[]{:S(2)}) async-start(), calls=%async_computation.3 | async-start | bytes 4456448 | tf_op jit(solution)/shard_map/reduce_scatter | solution.py:84
  12.8 73.2 %copy-start.4 = (bf16[192,512]{1,0:T(8,128)(2,1)S(1)}, bf16[192,512]{1,0:T(8,128)(2,1)}, u32[]{:S(2)}) copy-start(bf16[192,512]{1,0:T(8,128)(2,1)} %param.12) | copy-start | bytes 589828
  12.8 155.4 %copy-start.1 = (f32[1,256,512]{2,1,0:T(8,128)S(1)}, f32[1,256,512]{2,1,0:T(8,128)}, u32[]{:S(2)}) copy-start(f32[1,256,512]{2,1,0:T(8,128)} %param.14) | copy-start | bytes 1572868
  12.8 160.3 %copy-start.3 = (s32[1,32,512]{2,1,0:T(8,128)S(1)}, s32[1,32,512]{2,1,0:T(8,128)}, u32[]{:S(2)}) copy-start(s32[1,32,512]{2,1,0:T(8,128)} %param.15) | copy-start | bytes 196612
  176.3 48.4 %all-to-all-start = ((bf16[32,1,1,32,512]{4,3,2,1,0:T(8,128)(2,1)}), bf16[32,1,1,32,512]{4,3,2,1,0:T(8,128)(2,1)}, u32[]{:S(2)}, u32[]{:S(2)}) async-start(bf16[32,1,1,32,512]{4,3,2,1,0:T(8,128)(2,1)} %stack.3), calls=%async_computation.1 | async-start | bytes 2097152 | tf_op jit(solution)/shard_map/all_to_all | solution.py:14
  196.5 3.1 %copy-start.2 = (bf16[256,512]{1,0:T(8,128)(2,1)S(1)}, bf16[256,512]{1,0:T(8,128)(2,1)}, u32[]{:S(2)}) copy-start(bf16[256,512]{1,0:T(8,128)(2,1)} %reduce-scatter.2.cloned.1.call-done) | copy-start | bytes 786436
Sparse Core Ops, SparseCore 0:
  10.1 75.8 all-gather.1
  88.9 79.2 reduce-scatter.1
